TPU v7x, 256 devices: a whole 4x4x8 slice. The times are simulated.
256 devices in a mesh: gx: 16 (over z, x_hi), gy: 16 (over x_lo, y, core).
Axes of the slice: x: 4 (x_hi: 2, x_lo: 2; x = x_hi * 2 + x_lo), y: 4, z: 8, core: 2. Of those that a mesh axis runs over, the one named last changes fastest.
Arguments:
- tokens: bfloat16 [4096, 4096], P('gy', 'gx'), may hold values from -6 to 6
- attn_gain: bfloat16 [4096], replicated, may hold values from 0.099609375 to 1.8984375
- qkv_weight: bfloat16 [4096, 6144], P('gy', 'gx'), may hold values from -0.1875 to 0.1875
- out_weight: bfloat16 [4096, 4096], P('gx', 'gy'), may hold values from -0.09375 to 0.09375
- mlp_gain: bfloat16 [4096], replicated, may hold values from 0.099609375 to 1.8984375
- up_weight: bfloat16 [4096, 12288], P('gy', 'gx'), may hold values from -0.09375 to 0.09375
- down_weight: bfloat16 [12288, 4096], P('gx', 'gy'), may hold values from -0.0546875 to 0.0546875
- final_gain: bfloat16 [4096], replicated, may hold values from 0.099609375 to 1.8984375
- head_weight: bfloat16 [4096, 131072], P(None, ('gx', 'gy')), may hold values from -0.25 to 0.25
- kv_cache: bfloat16 [256, 4096, 256], P(('gy', 'gx')), may hold values from -40 to 40
- cache_lengths: int32 [32], replicated, may hold values from 1 to 3968, as said below
- slot_request: int32 [32], replicated, may hold values from 0 to 31, each once
Outputs:
- hidden_out: bfloat16 [4096, 4096], P('gy', 'gx')
- new_cache: bfloat16 [256, 4096, 256], P(('gy', 'gx'))
- last_norms: float32 [32], replicated
- max_logits: float32 [32], replicated
- head_input: bfloat16 [32, 4096], replicated
Inputs may be any that keep to these rules, and one draw needn't show every extreme that they name: `cache_lengths`: the longest request has exactly 3968 cached positions.
All inputs are finite; a program needn't handle non-finite values.
Results may differ from a plain program's by a relative error of at most 0.02.
The roundings to bfloat16 on the way count: a program that leaves them out, or rounds other values in their place, can miss the bound.
Values may be sent and summed in bfloat16 or wider, within the bound.
A program may use at most 128 MiB of HBM per device.

v0:
```python
import math
import jax
import jax.numpy as jnp
from jax import lax
from jax.sharding import PartitionSpec as P

HEADS = 32
KVH = 8
HD = 128
epsilon = 1e-05
negative = -1e30


def from_partner(block, axis, distance):
    count = lax.axis_size(axis)
    route = []
    for low in range(count):
        high = low | 1 << distance
        if high != low and high < count:
            route += [(low, high), (high, low)]
    return lax.ppermute(block, axis, route)


def rms_factor(row_block):
    return lax.rsqrt(jnp.mean(row_block * row_block, axis=-1, keepdims=True) + epsilon)


def gather_features(shard_rows):
    return lax.all_gather(shard_rows, "gx", axis=1, tiled=True)


def rows_product(left_rows, weight_shard):
    return jnp.dot(
        left_rows,
        lax.all_gather(weight_shard, "gy", axis=0, tiled=True),
        preferred_element_type=jnp.float32,
    )


def columns_product(left_rows, weight_shard):
    return jnp.dot(
        left_rows,
        lax.all_gather(weight_shard, "gy", axis=1, tiled=True),
        preferred_element_type=jnp.float32,
    )


def pair_swap(values):
    return from_partner(values, "gx", KVH.bit_length() - 1)


def scatter_partials(partial_terms):
    return lax.psum_scatter(
        partial_terms.astype(jnp.bfloat16), "gx", scatter_dimension=1, tiled=True
    ).astype(jnp.float32)


def merge_block(carried, scores, value_rows):
    row_max, running, numerator = carried
    new_max = jnp.maximum(row_max, jnp.max(scores, axis=1, keepdims=True))
    factor = jnp.exp(row_max - new_max)
    weights = jnp.exp(scores - new_max)
    running = running * factor + jnp.sum(weights, axis=1, keepdims=True)
    numerator = numerator * factor + jnp.dot(
        weights.astype(jnp.bfloat16), value_rows, preferred_element_type=jnp.float32
    )
    return (new_max, running, numerator)


def attend_cache(group_cols, cache_rows, length, new_rows):
    per_group = HEADS // KVH
    scaling = 1.0 / math.sqrt(HD)
    query_rows = per_group * new_rows
    queries = (
        group_cols[:, : per_group * HD]
        .reshape(new_rows, per_group, HD)
        .transpose(1, 0, 2)
        .reshape(query_rows, HD)
    )
    key_new = group_cols[:, per_group * HD : (per_group + 1) * HD]
    value_new = group_cols[:, (per_group + 1) * HD :]
    block_len = min(512, cache_rows.shape[0])

    def visit_block(step_index, carried):
        offset = step_index * block_len
        block_rows = lax.dynamic_slice_in_dim(cache_rows, offset, block_len, 0)
        scores = (
            jnp.dot(queries, block_rows[:, :HD].T, preferred_element_type=jnp.float32) * scaling
        )
        positions = offset + jnp.arange(block_len)
        scores = jnp.where(positions[None, :] < length, scores, negative)
        return merge_block(carried, scores, block_rows[:, HD:])

    initial = (
        jnp.full((query_rows, 1), negative, jnp.float32),
        jnp.zeros((query_rows, 1), jnp.float32),
        jnp.zeros((query_rows, HD), jnp.float32),
    )
    block_count = (length + block_len - 1) // block_len
    carried = lax.fori_loop(0, block_count, visit_block, initial)
    new_scores = jnp.dot(queries, key_new.T, preferred_element_type=jnp.float32) * scaling
    causal = jnp.arange(new_rows)[None, :] <= (jnp.arange(query_rows) % new_rows)[:, None]
    new_scores = jnp.where(causal, new_scores, negative)
    row_max, running, numerator = merge_block(carried, new_scores, value_new)
    attended = (numerator / running).astype(jnp.bfloat16)
    attended = (
        attended.reshape(per_group, new_rows, HD)
        .transpose(1, 0, 2)
        .reshape(new_rows, per_group * HD)
    )
    fresh = jnp.concatenate([key_new, value_new], axis=1)
    appended = lax.dynamic_update_slice(cache_rows, fresh, (length, jnp.zeros((), jnp.int32)))
    return (attended, appended)


def local(
    tokens,
    attn_gain,
    qkv_weight,
    out_weight,
    mlp_gain,
    up_weight,
    down_weight,
    final_gain,
    head_weight,
    kv_cache,
    cache_lengths,
    slot_request,
):
    gx_count = lax.axis_size("gx")
    gy_count = lax.axis_size("gy")
    copies = gx_count // KVH
    gx_place = lax.axis_index("gx")
    copy_index = gx_place // KVH
    slot_index = lax.axis_index("gy") * copies + copy_index
    new_rows = tokens.shape[0] // copies
    feature_cols = tokens.shape[1]
    gathered_tokens = gather_features(tokens)
    tokens_f32 = gathered_tokens.astype(jnp.float32)
    normed = (tokens_f32 * rms_factor(tokens_f32) * attn_gain.astype(jnp.float32)).astype(
        jnp.bfloat16
    )
    projected = rows_product(normed, qkv_weight).astype(jnp.bfloat16)
    own_half = lax.dynamic_slice_in_dim(projected, copy_index * new_rows, new_rows, 0)
    sent_rows = lax.dynamic_slice_in_dim(projected, (1 - copy_index) * new_rows, new_rows, 0)
    received = pair_swap(sent_rows)
    group_cols = jnp.where(
        copy_index == 0,
        jnp.concatenate([own_half, received], axis=1),
        jnp.concatenate([received, own_half], axis=1),
    )
    length = cache_lengths[slot_request[slot_index]]
    attended, appended = attend_cache(group_cols, kv_cache[0], length, new_rows)
    new_cache = appended[None]
    half_width = attended.shape[1] // 2
    kept_half = lax.dynamic_slice_in_dim(attended, copy_index * half_width, half_width, 1)
    handed = lax.dynamic_slice_in_dim(attended, (1 - copy_index) * half_width, half_width, 1)
    returned = pair_swap(handed)
    attention_rows = jnp.where(
        copy_index == 0,
        jnp.concatenate([kept_half, returned], axis=0),
        jnp.concatenate([returned, kept_half], axis=0),
    )
    attention_terms = columns_product(attention_rows, out_weight)
    middle = (tokens.astype(jnp.float32) + scatter_partials(attention_terms)).astype(jnp.bfloat16)
    middle_full = gather_features(middle)
    middle_f32 = middle_full.astype(jnp.float32)
    mlp_input = (middle_f32 * rms_factor(middle_f32) * mlp_gain.astype(jnp.float32)).astype(
        jnp.bfloat16
    )
    up_values = rows_product(mlp_input, up_weight)
    rectified = jnp.maximum(up_values, 0.0)
    activation = (rectified * rectified).astype(jnp.bfloat16)
    down_terms = columns_product(activation, down_weight)
    hidden_out = (middle.astype(jnp.float32) + scatter_partials(down_terms)).astype(jnp.bfloat16)
    final_rows = hidden_out.reshape(copies, new_rows, feature_cols)[:, new_rows - 1, :]
    every_last = lax.all_gather(final_rows, ("gx", "gy"), axis=0, tiled=True)
    slot_rows = every_last.reshape(gx_count, gy_count, copies, feature_cols).transpose(1, 2, 0, 3)
    slot_rows = slot_rows.reshape(gy_count * copies, gx_count * feature_cols).astype(jnp.float32)
    mean_square = jnp.mean(slot_rows * slot_rows, axis=1)
    last_norms = jnp.sqrt(mean_square)
    head_input = (
        slot_rows * lax.rsqrt(mean_square + epsilon)[:, None] * final_gain.astype(jnp.float32)
    ).astype(jnp.bfloat16)
    logits = jnp.dot(head_input, head_weight, preferred_element_type=jnp.float32)
    max_logits = lax.pmax(jnp.max(logits, axis=1), ("gx", "gy"))
    return (hidden_out, new_cache, last_norms, max_logits, head_input)


def solution(mesh):
    in_specs = (
        P("gy", "gx"),
        P(),
        P("gy", "gx"),
        P("gx", "gy"),
        P(),
        P("gy", "gx"),
        P("gx", "gy"),
        P(),
        P(None, ("gx", "gy")),
        P(("gy", "gx"), None, None),
        P(),
        P(),
    )
    out_specs = (P("gy", "gx"), P(("gy", "gx"), None, None), P(), P(), P())
    return jax.shard_map(local, mesh=mesh, in_specs=in_specs, out_specs=out_specs, check_vma=False)
```

profile of v0, /device:TPU:1, one launch (start us, length us, event | category | flops | bytes accessed | tf_op | source)
XLA Modules:
  0.0 957.5 jit_solution(2756551729727596490)
XLA Ops:
  7.2 0.7 all-gather.8.cloned.1.call-update
  8.0 0.7 all-gather.10.cloned.1.call-update
  8.7 0.7 all-gather.12.cloned.1.call-update
  9.5 0.6 dynamic_slice.21
  12.0 0.6 dynamic_slice.22
  13.4 81.3 %all-gather.8.cloned.1.call-done = bf16[256,4096]{1,0:T(8,128)(2,1)} async-done(((bf16[256,256]{1,0:T(8,128)(2,1)}), bf16[256,4096]{1,0:T(8,128)(2,1)}) %all-gather.8.cloned.1.call-update) | async-done | bytes 2097168 | tf_op jit(solution)/shard_map/all_gather | solution.py:29
  94.6 2.1 fusion.8
  96.7 39.1 %all-gather.10.cloned.1.call-done = bf16[4096,384]{1,0:T(8,128)(2,1)} async-done(((bf16[256,384]{1,0:T(8,128)(2,1)}), bf16[4096,384]{1,0:T(8,128)(2,1)}) %all-gather.10.cloned.1.call-update) | async-done | bytes 3145744 | tf_op jit(solution)/shard_map/all_gather | solution.py:35
  135.8 3.8 fusion.31
  139.7 5.5 collective-permute-start
  145.2 2.7 collective-permute-done
  148.0 1.5 fusion.58
  149.6 4.9 while.14
  149.6 0.7 add_compare_fusion.2
  150.3 0.3 fusion.75
  150.8 0.4 convolution_add_fusion.3
  151.2 0.7 add_compare_fusion.2
  151.9 0.3 fusion.75
  152.5 0.4 convolution_add_fusion.3
  152.9 0.7 add_compare_fusion.2
  153.6 0.3 fusion.75
  154.1 0.4 convolution_add_fusion.3
  154.5 0.7 max.14
  155.2 1.0 fusion.40
  156.2 1.2 fusion.36
  157.6 5.5 collective-permute-start.1
  163.2 14.0 %all-gather.12.cloned.1.call-done = bf16[256,4096]{1,0:T(8,128)(2,1)} async-done(((bf16[256,256]{1,0:T(8,128)(2,1)}), bf16[256,4096]{1,0:T(8,128)(2,1)}) %all-gather.12.cloned.1.call-update) | async-done | bytes 2097168 | tf_op jit(solution)/shard_map/all_gather | solution.py:43
  177.2 3.7 convolution_convert_fusion
  180.9 205.0 %reduce-scatter.3.cloned.1.call-done = bf16[256,256]{1,0:T(8,128)(2,1)} async-done(((bf16[256,4096]{1,0:T(8,128)(2,1)}), bf16[256,256]{1,0:T(8,128)(2,1)}) %reduce-scatter.3.cloned.1.call-update) | async-done | bytes 131088 | tf_op jit(solution)/shard_map/reduce_scatter | solution.py:53
  385.9 1.6 add_convert_fusion.1
  387.6 0.5 all-gather.16.cloned.1.call-update
  388.1 0.7 all-gather.18.cloned.1.call-update
  388.9 83.5 %all-gather.14.cloned.1.call-done = bf16[256,4096]{1,0:T(8,128)(2,1)} async-done(((bf16[256,256]{1,0:T(8,128)(2,1)}), bf16[256,4096]{1,0:T(8,128)(2,1)}) %all-gather.14.cloned.1.call-update) | async-done | bytes 2097168 | tf_op jit(solution)/shard_map/all_gather | solution.py:29
  472.4 2.1 fusion.11
  474.5 45.9 %all-gather.16.cloned.1.call-done = bf16[4096,768]{1,0:T(8,128)(2,1)} async-done(((bf16[256,768]{1,0:T(8,128)(2,1)}), bf16[4096,768]{1,0:T(8,128)(2,1)}) %all-gather.16.cloned.1.call-update) | async-done | bytes 6291472 | tf_op jit(solution)/shard_map/all_gather | solution.py:35
  520.4 58.7 %all-gather.18.cloned.1.call-done = bf16[768,4096]{1,0:T(8,128)(2,1)} async-done(((bf16[768,256]{1,0:T(8,128)(2,1)}), bf16[768,4096]{1,0:T(8,128)(2,1)}) %all-gather.18.cloned.1.call-update) | async-done | bytes 6291472 | tf_op jit(solution)/shard_map/all_gather | solution.py:43
  579.0 11.1 %convolution_convert_fusion.1 = bf16[256,4096]{1,0:T(8,128)(2,1)} fusion(bf16[768,4096]{1,0:T(8,128)(2,1)} %all-gather.18.cloned.1.call-done, bf16[4096,768]{1,0:T(8,128)(2,1)} %all-gather.16.cloned.1.call-done, bf16[256,4096]{1,0:T(8,128)(2,1)} %all-gather.14.cloned.1.call-done, f32[4096]{0:T(1024)S(1)} %convert_element_type.90, f32[256]{0:T(256)S(1)} %add_rsqrt_fusion.1), kind=kOutput, calls=%fused_computation.18 | convolution fusion | flops 3227058176 | bytes 16794624 | tf_op jit(solution)/shard_map/dot_general | solution.py:41
  592.2 0.8 slice_bitcast_fusion
  593.0 201.4 %reduce-scatter.5.cloned.1.call-done = bf16[256,256]{1,0:T(8,128)(2,1)} async-done(((bf16[256,4096]{1,0:T(8,128)(2,1)}), bf16[256,256]{1,0:T(8,128)(2,1)}) %reduce-scatter.5.cloned.1.call-update) | async-done | bytes 131088 | tf_op jit(solution)/shard_map/reduce_scatter | solution.py:53
  794.4 0.9 add_convert_fusion
  795.4 72.9 %all-gather = bf16[512,1,256]{2,1,0:T(2,128)(2,1)S(1)} all-gather(bf16[2,1,256]{2,1,0:T(2,128)(2,1)S(1)} %slice.26), channel_id=2, replica_groups=mesh['gx'=16,'gy'=16] {'gx','gy'}, dimensions={0}, use_global_device_ids=true | all-gather | bytes 263168 | tf_op jit(solution)/shard_map/all_gather | solution.py:177
  868.3 2.2 convert_reduce_fusion
  870.9 0.3 copy.24
  871.2 0.3 copy.26
  871.9 3.2 convolution_reduce_fusion
  875.1 0.6 dynamic_update_slice.4
  875.8 74.3 %pmax.7 = f32[32]{0:T(128)} all-reduce(f32[32]{0:T(128)S(1)} %convolution_reduce_fusion), channel_id=1, replica_groups=mesh['gx'=16,'gy'=16] {'gx','gy'}, use_global_device_ids=true, to_apply=%region_13.14 | all-reduce | flops 32 | bytes 256 | tf_op jit(solution)/shard_map/pmax | solution.py:186
  950.0 0.6 sqrt.7
  (72 shorter events, 2.2 us)
Async XLA Ops:
  7.2 6.1 copy-start.7
  7.2 4.9 copy-start.11
  7.2 2.3 copy-start.10
  7.2 87.4 %all-gather.8.cloned.1.call-start = ((), (), s32[]{:S(2)}) async-start(), calls=%async_computation.2 | async-start | bytes 2228224 | tf_op jit(solution)/shard_map/all_gather | solution.py:29
  7.9 127.9 %all-gather.10.cloned.1.call-start = ((), (), s32[]{:S(2)}) async-start(), calls=%async_computation.3 | async-start | bytes 3342336 | tf_op jit(solution)/shard_map/all_gather | solution.py:35
  8.7 168.5 %all-gather.12.cloned.1.call-start = ((), (), s32[]{:S(2)}) async-start(), calls=%async_computation.4 | async-start | bytes 2228224 | tf_op jit(solution)/shard_map/all_gather | solution.py:43
  9.4 376.5 %reduce-scatter.3.cloned.1.call-start = ((), (), s32[]{:S(2)}) async-start(), calls=%async_computation.5 | async-start | bytes 2228224 | tf_op jit(solution)/shard_map/reduce_scatter | solution.py:53
  96.7 52.8 %copy-start.1 = (bf16[1,4096,256]{2,1,0:T(8,128)(2,1)S(1)}, bf16[1,4096,256]{2,1,0:T(8,128)(2,1)}, u32[]{:S(2)}) copy-start(bf16[1,4096,256]{2,1,0:T(8,128)(2,1)} %param.23) | copy-start | bytes 6291460
  139.7 8.2 collective-permute-start
  148.0 1.6 copy-start.4
  157.6 19.5 %collective-permute-start.1 = (bf16[128,256]{0,1:T(8,128)(2,1)S(1)}, bf16[128,256]{0,1:T(8,128)(2,1)S(1)}, u32[]{:S(2)}, u32[]{:S(2)}) collective-permute-start(bf16[128,256]{0,1:T(8,128)(2,1)S(1)} %get-tuple-element.80), channel_id=1, source_target_pairs={{0,128},{128,0},{16,144},{144,16},{32,160},{160,32},{48,176},{176,... | collective-permute-start | bytes 196616 | tf_op jit(solution)/shard_map/ppermute | solution.py:21
  177.1 208.7 %copy-start.5 = (bf16[256,256]{1,0:T(8,128)(2,1)S(1)}, bf16[256,256]{1,0:T(8,128)(2,1)}, u32[]{:S(2)}) copy-start(bf16[256,256]{1,0:T(8,128)(2,1)} %param.14) | copy-start | bytes 393220
  177.1 211.7 %copy-start.8 = (bf16[4096]{0:T(1024)(128)(2,1)S(1)}, bf16[4096]{0:T(1024)(128)(2,1)}, u32[]{:S(2)}) copy-start(bf16[4096]{0:T(1024)(128)(2,1)} %param.18) | copy-start | bytes 24580
  180.9 291.5 %all-gather.14.cloned.1.call-start = ((), (), s32[]{:S(2)}) async-start(), calls=%async_computation.6 | async-start | bytes 2228224 | tf_op jit(solution)/shard_map/all_gather | solution.py:29
  387.5 132.8 %all-gather.16.cloned.1.call-start = ((), (), s32[]{:S(2)}) async-start(), calls=%async_computation.7 | async-start | bytes 6684672 | tf_op jit(solution)/shard_map/all_gather | solution.py:35
  388.1 190.9 %all-gather.18.cloned.1.call-start = ((), (), s32[]{:S(2)}) async-start(), calls=%async_computation.8 | async-start | bytes 6684672 | tf_op jit(solution)/shard_map/all_gather | solution.py:43
  388.8 405.6 %reduce-scatter.5.cloned.1.call-start = ((), (), s32[]{:S(2)}) async-start(), calls=%async_computation.9 | async-start | bytes 2228224 | tf_op jit(solution)/shard_map/reduce_scatter | solution.py:53
  474.5 117.0 %copy-start.9 = (bf16[4096]{0:T(1024)(128)(2,1)S(1)}, bf16[4096]{0:T(1024)(128)(2,1)}, u32[]{:S(2)}) copy-start(bf16[4096]{0:T(1024)(128)(2,1)} %param.21) | copy-start | bytes 24580
  474.5 320.0 %copy-start.2 = (bf16[256,256]{1,0:T(8,128)(2,1)S(1)}, bf16[256,256]{1,0:T(8,128)(2,1)}, u32[]{:S(2)}) copy-start(bf16[256,256]{1,0:T(8,128)(2,1)} %add_convert_fusion.1) | copy-start | bytes 393220
  795.4 79.8 %copy-start.6 = (bf16[256,256]{1,0:T(8,128)(2,1)}, bf16[256,256]{1,0:T(8,128)(2,1)S(1)}, u32[]{:S(2)}) copy-start(bf16[256,256]{1,0:T(8,128)(2,1)S(1)} %add_convert_fusion) | copy-start | bytes 393220
  871.9 78.7 %copy-start.3 = (bf16[32,4096]{1,0:T(8,128)(2,1)}, bf16[32,4096]{1,0:T(8,128)(2,1)S(1)}, u32[]{:S(2)}) copy-start(bf16[32,4096]{1,0:T(8,128)(2,1)S(1)} %multiply_convert_fusion) | copy-start | bytes 786436
  875.8 74.9 %copy-start = (bf16[1,4096,256]{2,1,0:T(8,128)(2,1)}, bf16[1,4096,256]{2,1,0:T(8,128)(2,1)S(1)}, u32[]{:S(2)}) copy-start(bf16[1,4096,256]{2,1,0:T(8,128)(2,1)S(1)} %dynamic_update_slice.4) | copy-start | bytes 6291460
Sparse Core Ops, SparseCore 0:
  10.5 84.1 all-gather.7
  96.5 39.2 all-gather.9
  137.6 39.5 all-gather.11
  181.5 204.3 reduce-scatter.2
  388.8 83.5 all-gather.13
  474.1 46.2 all-gather.15
  522.1 56.8 all-gather.17
  590.3 204.0 reduce-scatter.4
where the time goes:
time: 958 us; the launch traced here: 957 us
  waiting for transfers between devices  735 us (77%)
  blocking collectives  147 us (15%)
  matrix products  26.7 us (3%)
  between operations  19.1 us (2%)
  other arithmetic  13.5 us (1%)
  starting transfers between devices  11.4 us (1%)
    reduce_scatter x2, waiting for transfers between devices, scatter_partials(): lax.psum_scatter(partial_terms.astype(jnp.bfloat16), 'gx', scatter_dimens...  406 us
    all_gather x2, waiting for transfers between devices, gather_features(): return lax.all_gather(shard_rows, 'gx', axis=1, tiled=True)  165 us
    all_gather x2, waiting for transfers between devices, rows_product(): lax.all_gather(weight_shard, 'gy', axis=0, tiled=True)  84.9 us
    pmax x1, blocking collectives, local(): max_logits = lax.pmax(jnp.max(logits, axis=1), ('gx', 'gy'))  74.3 us
    all_gather x1, blocking collectives, local(): every_last = lax.all_gather(final_rows, ('gx', 'gy'), axis=0, tiled=True)  72.9 us
    all_gather x2, waiting for transfers between devices, columns_product(): lax.all_gather(weight_shard, 'gy', axis=1, tiled=True)  72.7 us
  transfers between devices with their start and end apart: 10, of which 9 were waited for; matrix products, arithmetic and copies ran while one was open for 2% of the time, Pallas kernels for 0%

commit v1 on v0

--- a/solution.py
+++ b/solution.py
@@ -174,7 +174,10 @@
     down_terms = columns_product(activation, down_weight)
     hidden_out = (middle.astype(jnp.float32) + scatter_partials(down_terms)).astype(jnp.bfloat16)
     final_rows = hidden_out.reshape(copies, new_rows, feature_cols)[:, new_rows - 1, :]
-    every_last = lax.all_gather(final_rows, ("gx", "gy"), axis=0, tiled=True)
+    every_last = jnp.concatenate(
+        lax.all_to_all(jnp.stack([final_rows] * lax.axis_size(("gx", "gy"))), ("gx", "gy"), 0, 0),
+        axis=0,
+    )
     slot_rows = every_last.reshape(gx_count, gy_count, copies, feature_cols).transpose(1, 2, 0, 3)
     slot_rows = slot_rows.reshape(gy_count * copies, gx_count * feature_cols).astype(jnp.float32)
     mean_square = jnp.mean(slot_rows * slot_rows, axis=1)

time: 958 us -> 912 us (0.952)
  blocking collectives: 147 us -> 72.6 us
  waiting for transfers between devices: 735 us -> 750 us
  starting transfers between devices: 11.4 us -> 26.4 us
    all_gather x1 -> x0, blocking collectives: 72.9 us -> none  [local(): every_last = lax.all_gather(final_rows, ('gx', 'gy'), axis=0, tiled=True)]
    all_to_all x0 -> x1, starting transfers between devices: none -> 15 us  [local(): lax.all_to_all(jnp.stack([final_rows] * lax.axis_size(('gx', 'gy'))), ('g...]
    all_to_all x0 -> x1, waiting for transfers between devices: none -> 12.5 us  [local(): lax.all_to_all(jnp.stack([final_rows] * lax.axis_size(('gx', 'gy'))), ('g...]
  transfers between devices with their start and end apart: 10 -> 11, of which waited for: 9 -> 10; matrix products, arithmetic and copies ran while one was open for 2% -> 2% of each run, Pallas kernels for 0% -> 0%
where the time goes in v1:
time: 912 us
  waiting for transfers between devices  750 us (82%)
  blocking collectives  72.6 us (8%)
  matrix products  26.7 us (3%)
  starting transfers between devices  26.4 us (3%)
  between operations  19.1 us (2%)
  other arithmetic  11.5 us (1%)
    reduce_scatter x2, waiting for transfers between devices, scatter_partials(): lax.psum_scatter(partial_terms.astype(jnp.bfloat16), 'gx', scatter_dimens...  409 us
    all_gather x2, waiting for transfers between devices, gather_features(): return lax.all_gather(shard_rows, 'gx', axis=1, tiled=True)  165 us
    all_gather x2, waiting for transfers between devices, rows_product(): lax.all_gather(weight_shard, 'gy', axis=0, tiled=True)  84.9 us
    all_gather x2, waiting for transfers between devices, columns_product(): lax.all_gather(weight_shard, 'gy', axis=1, tiled=True)  72.7 us
    pmax x1, blocking collectives, local(): max_logits = lax.pmax(jnp.max(logits, axis=1), ('gx', 'gy'))  72.6 us
  transfers between devices with their start and end apart: 11, of which 10 were waited for; matrix products, arithmetic and copies ran while one was open for 2% of the time, Pallas kernels for 0%

profile of v1, /device:TPU:1, one launch (start us, length us, event | category | flops | bytes accessed | tf_op | source)
XLA Modules:
  0.0 911.8 jit_solution(16123884641705987061)
XLA Ops:
  7.2 0.7 all-gather.7.cloned.1.call-update
  8.0 0.7 all-gather.9.cloned.1.call-update
  8.7 0.7 all-gather.11.cloned.1.call-update
  9.5 0.6 dynamic_slice.21
  12.0 0.6 dynamic_slice.22
  13.4 81.3 %all-gather.7.cloned.1.call-done = bf16[256,4096]{1,0:T(8,128)(2,1)} async-done(((bf16[256,256]{1,0:T(8,128)(2,1)}), bf16[256,4096]{1,0:T(8,128)(2,1)}) %all-gather.7.cloned.1.call-update) | async-done | bytes 2097168 | tf_op jit(solution)/shard_map/all_gather | solution.py:29
  94.6 2.1 fusion.8
  96.7 39.1 %all-gather.9.cloned.1.call-done = bf16[4096,384]{1,0:T(8,128)(2,1)} async-done(((bf16[256,384]{1,0:T(8,128)(2,1)}), bf16[4096,384]{1,0:T(8,128)(2,1)}) %all-gather.9.cloned.1.call-update) | async-done | bytes 3145744 | tf_op jit(solution)/shard_map/all_gather | solution.py:35
  135.8 3.8 fusion.31
  139.7 5.5 collective-permute-start
  145.2 2.7 collective-permute-done
  148.0 1.5 fusion.58
  149.6 4.9 while.14
  149.6 0.7 add_compare_fusion.2
  150.3 0.3 fusion.75
  150.8 0.4 convolution_add_fusion.3
  151.2 0.7 add_compare_fusion.2
  151.9 0.3 fusion.75
  152.5 0.4 convolution_add_fusion.3
  152.9 0.7 add_compare_fusion.2
  153.6 0.3 fusion.75
  154.1 0.4 convolution_add_fusion.3
  154.5 0.7 max.14
  155.2 1.0 fusion.40
  156.2 1.2 fusion.36
  157.6 5.5 collective-permute-start.1
  163.2 14.0 %all-gather.11.cloned.1.call-done = bf16[256,4096]{1,0:T(8,128)(2,1)} async-done(((bf16[256,256]{1,0:T(8,128)(2,1)}), bf16[256,4096]{1,0:T(8,128)(2,1)}) %all-gather.11.cloned.1.call-update) | async-done | bytes 2097168 | tf_op jit(solution)/shard_map/all_gather | solution.py:43
  177.2 3.7 convolution_convert_fusion
  180.9 205.0 %reduce-scatter.3.cloned.1.call-done = bf16[256,256]{1,0:T(8,128)(2,1)} async-done(((bf16[256,4096]{1,0:T(8,128)(2,1)}), bf16[256,256]{1,0:T(8,128)(2,1)}) %reduce-scatter.3.cloned.1.call-update) | async-done | bytes 131088 | tf_op jit(solution)/shard_map/reduce_scatter | solution.py:53
  385.9 1.6 add_convert_fusion.1
  387.6 0.5 all-gather.15.cloned.1.call-update
  388.1 0.7 all-gather.17.cloned.1.call-update
  388.9 83.5 %all-gather.13.cloned.1.call-done = bf16[256,4096]{1,0:T(8,128)(2,1)} async-done(((bf16[256,256]{1,0:T(8,128)(2,1)}), bf16[256,4096]{1,0:T(8,128)(2,1)}) %all-gather.13.cloned.1.call-update) | async-done | bytes 2097168 | tf_op jit(solution)/shard_map/all_gather | solution.py:29
  472.4 2.1 fusion.11
  474.5 45.9 %all-gather.15.cloned.1.call-done = bf16[4096,768]{1,0:T(8,128)(2,1)} async-done(((bf16[256,768]{1,0:T(8,128)(2,1)}), bf16[4096,768]{1,0:T(8,128)(2,1)}) %all-gather.15.cloned.1.call-update) | async-done | bytes 6291472 | tf_op jit(solution)/shard_map/all_gather | solution.py:35
  520.4 58.7 %all-gather.17.cloned.1.call-done = bf16[768,4096]{1,0:T(8,128)(2,1)} async-done(((bf16[768,256]{1,0:T(8,128)(2,1)}), bf16[768,4096]{1,0:T(8,128)(2,1)}) %all-gather.17.cloned.1.call-update) | async-done | bytes 6291472 | tf_op jit(solution)/shard_map/all_gather | solution.py:43
  579.0 11.1 %convolution_convert_fusion.1 = bf16[256,4096]{1,0:T(8,128)(2,1)} fusion(bf16[768,4096]{1,0:T(8,128)(2,1)} %all-gather.17.cloned.1.call-done, bf16[4096,768]{1,0:T(8,128)(2,1)} %all-gather.15.cloned.1.call-done, bf16[256,4096]{1,0:T(8,128)(2,1)} %all-gather.13.cloned.1.call-done, f32[4096]{0:T(1024)S(1)} %convert_element_type.90, f32[256]{0:T(256)S(1)} %add_rsqrt_fusion.1), kind=kOutput, calls=%fused_computation.18 | convolution fusion | flops 3227058176 | bytes 16794624 | tf_op jit(solution)/shard_map/dot_general | solution.py:41
  590.2 204.2 %reduce-scatter.5.cloned.1.call-done = bf16[256,256]{1,0:T(8,128)(2,1)} async-done(((bf16[256,4096]{1,0:T(8,128)(2,1)}), bf16[256,256]{1,0:T(8,128)(2,1)}) %reduce-scatter.5.cloned.1.call-update) | async-done | bytes 131088 | tf_op jit(solution)/shard_map/reduce_scatter | solution.py:53
  794.4 0.9 add_convert_fusion
  795.4 0.8 stack.3
  796.3 15.0 %all-to-all-start = ((bf16[256,2,256]{2,1,0:T(2,128)(2,1)}), bf16[256,2,256]{2,1,0:T(2,128)(2,1)S(1)}, u32[]{:S(2)}, u32[]{:S(2)}) async-start(bf16[256,2,256]{2,1,0:T(2,128)(2,1)} %stack.3), calls=%async_computation.2 | async-start | bytes 524288 | tf_op jit(solution)/shard_map/all_to_all | solution.py:178
  813.2 0.8 slice_bitcast_fusion
  814.1 12.5 %all-to-all-done = bf16[256,2,256]{2,1,0:T(2,128)(2,1)S(1)} async-done(((bf16[256,2,256]{2,1,0:T(2,128)(2,1)}), bf16[256,2,256]{2,1,0:T(2,128)(2,1)S(1)}, u32[]{:S(2)}, u32[]{:S(2)}) %all-to-all-start) | async-done | bytes 262176 | tf_op jit(solution)/shard_map/all_to_all | solution.py:178
  826.6 0.3 copy.35
  827.8 3.2 convolution_reduce_fusion
  831.0 0.6 dynamic_update_slice.4
  831.7 72.6 %pmax.7 = f32[32]{0:T(128)} all-reduce(f32[32]{0:T(128)S(1)} %convolution_reduce_fusion), channel_id=1, replica_groups=mesh['gx'=16,'gy'=16] {'gx','gy'}, use_global_device_ids=true, to_apply=%region_13.14 | all-reduce | flops 32 | bytes 256 | tf_op jit(solution)/shard_map/pmax | solution.py:189
  904.4 0.6 sqrt.7
  (77 shorter events, 2.5 us)
Async XLA Ops:
  7.2 6.1 copy-start.7
  7.2 4.9 copy-start.11
  7.2 2.3 copy-start.10
  7.2 87.4 %all-gather.7.cloned.1.call-start = ((), (), s32[]{:S(2)}) async-start(), calls=%async_computation.3 | async-start | bytes 2228224 | tf_op jit(solution)/shard_map/all_gather | solution.py:29
  7.9 127.9 %all-gather.9.cloned.1.call-start = ((), (), s32[]{:S(2)}) async-start(), calls=%async_computation.4 | async-start | bytes 3342336 | tf_op jit(solution)/shard_map/all_gather | solution.py:35
  8.7 168.5 %all-gather.11.cloned.1.call-start = ((), (), s32[]{:S(2)}) async-start(), calls=%async_computation.5 | async-start | bytes 2228224 | tf_op jit(solution)/shard_map/all_gather | solution.py:43
  9.4 376.5 %reduce-scatter.3.cloned.1.call-start = ((), (), s32[]{:S(2)}) async-start(), calls=%async_computation.6 | async-start | bytes 2228224 | tf_op jit(solution)/shard_map/reduce_scatter | solution.py:53
  96.7 52.8 %copy-start.1 = (bf16[1,4096,256]{2,1,0:T(8,128)(2,1)S(1)}, bf16[1,4096,256]{2,1,0:T(8,128)(2,1)}, u32[]{:S(2)}) copy-start(bf16[1,4096,256]{2,1,0:T(8,128)(2,1)} %param.23) | copy-start | bytes 6291460
  139.7 8.2 collective-permute-start
  148.0 1.6 copy-start.4
  157.6 19.5 %collective-permute-start.1 = (bf16[128,256]{0,1:T(8,128)(2,1)S(1)}, bf16[128,256]{0,1:T(8,128)(2,1)S(1)}, u32[]{:S(2)}, u32[]{:S(2)}) collective-permute-start(bf16[128,256]{0,1:T(8,128)(2,1)S(1)} %get-tuple-element.78), channel_id=1, source_target_pairs={{0,128},{128,0},{16,144},{144,16},{32,160},{160,32},{48,176},{176,... | collective-permute-start | bytes 196616 | tf_op jit(solution)/shard_map/ppermute | solution.py:21
  177.1 208.7 %copy-start.5 = (bf16[256,256]{1,0:T(8,128)(2,1)S(1)}, bf16[256,256]{1,0:T(8,128)(2,1)}, u32[]{:S(2)}) copy-start(bf16[256,256]{1,0:T(8,128)(2,1)} %param.14) | copy-start | bytes 393220
  177.1 211.7 %copy-start.8 = (bf16[4096]{0:T(1024)(128)(2,1)S(1)}, bf16[4096]{0:T(1024)(128)(2,1)}, u32[]{:S(2)}) copy-start(bf16[4096]{0:T(1024)(128)(2,1)} %param.18) | copy-start | bytes 24580
  180.9 291.5 %all-gather.13.cloned.1.call-start = ((), (), s32[]{:S(2)}) async-start(), calls=%async_computation.7 | async-start | bytes 2228224 | tf_op jit(solution)/shard_map/all_gather | solution.py:29
  387.5 132.8 %all-gather.15.cloned.1.call-start = ((), (), s32[]{:S(2)}) async-start(), calls=%async_computation.8 | async-start | bytes 6684672 | tf_op jit(solution)/shard_map/all_gather | solution.py:35
  388.1 190.9 %all-gather.17.cloned.1.call-start = ((), (), s32[]{:S(2)}) async-start(), calls=%async_computation.9 | async-start | bytes 6684672 | tf_op jit(solution)/shard_map/all_gather | solution.py:43
  388.8 405.6 %reduce-scatter.5.cloned.1.call-start = ((), (), s32[]{:S(2)}) async-start(), calls=%async_computation.10 | async-start | bytes 2228224 | tf_op jit(solution)/shard_map/reduce_scatter | solution.py:53
  474.5 320.0 %copy-start.2 = (bf16[256,256]{1,0:T(8,128)(2,1)S(1)}, bf16[256,256]{1,0:T(8,128)(2,1)}, u32[]{:S(2)}) copy-start(bf16[256,256]{1,0:T(8,128)(2,1)} %add_convert_fusion.1) | copy-start | bytes 393220
  590.2 222.4 %copy-start.9 = (bf16[4096]{0:T(1024)(128)(2,1)S(1)}, bf16[4096]{0:T(1024)(128)(2,1)}, u32[]{:S(2)}) copy-start(bf16[4096]{0:T(1024)(128)(2,1)} %param.21) | copy-start | bytes 24580
  795.4 0.9 copy-start.6
  796.3 30.3 %all-to-all-start = ((bf16[256,2,256]{2,1,0:T(2,128)(2,1)}), bf16[256,2,256]{2,1,0:T(2,128)(2,1)S(1)}, u32[]{:S(2)}, u32[]{:S(2)}) async-start(bf16[256,2,256]{2,1,0:T(2,128)(2,1)} %stack.3), calls=%async_computation.2 | async-start | bytes 524288 | tf_op jit(solution)/shard_map/all_to_all | solution.py:178
  827.8 77.2 %copy-start.3 = (bf16[32,4096]{1,0:T(8,128)(2,1)}, bf16[32,4096]{1,0:T(8,128)(2,1)S(1)}, u32[]{:S(2)}) copy-start(bf16[32,4096]{1,0:T(8,128)(2,1)S(1)} %multiply_convert_fusion) | copy-start | bytes 786436
  831.7 73.3 %copy-start = (bf16[1,4096,256]{2,1,0:T(8,128)(2,1)}, bf16[1,4096,256]{2,1,0:T(8,128)(2,1)S(1)}, u32[]{:S(2)}) copy-start(bf16[1,4096,256]{2,1,0:T(8,128)(2,1)S(1)} %dynamic_update_slice.4) | copy-start | bytes 6291460
Sparse Core Ops, SparseCore 0:
  10.5 84.1 all-gather.6
  96.5 39.2 all-gather.8
  137.6 39.5 all-gather.10
  181.5 204.3 reduce-scatter.2
  388.8 83.5 all-gather.12
  474.1 46.2 all-gather.14
  522.1 56.8 all-gather.16
  590.3 204.0 reduce-scatter.4
